TPU v7x, 32 devices: a whole 2x2x4 slice. The times are simulated.
32 devices in a mesh: blk: 16 (over z, x, core), feat: 2 (over y).
Axes of the slice: x: 2, y: 2, z: 4, core: 2. Of those that a mesh axis runs over, the one named last changes fastest.
Arguments:
- inputs: bfloat16 [4096, 1024], P('blk'), may hold values from -6 to 6
- col_mask: int32 [2, 1024], replicated, may hold values 0 or 1
- row_mask: int32 [4096], P('blk'), may hold values from 0 to 1
- width_class: int32 [4096], P('blk'), may hold values from 0 to 1
- frequencies: bfloat16 [2048, 2048], P(None, 'feat'), may hold values from -0.375 to 0.375
- phases: float32 [2048], P('feat'), may hold values from -3.140625 to 3.140625
- targets: float32 [4096], P('blk'), may hold values from -6 to 6
- prior_draws: float32 [4096, 16], P('blk'), may hold values from -6 to 6
- hidden_weight: float32 [1024, 2048], P('blk', 'feat'), may hold values from -0.1875 to 0.1875
- hidden_moment: float32 [1024, 2048], P('blk', 'feat'), may hold values from -9.536743e-06 to 9.536743e-06
- hidden_second: float32 [1024, 2048], P('blk', 'feat'), may hold values from 4.2e-14 to 1.7e-13
- alpha_weight: float32 [4096, 16], P('blk'), may hold values from -1.5 to 1.5
- alpha_moment: float32 [4096, 16], P('blk'), may hold values from -2.2888184e-05 to 2.2888184e-05
- alpha_second: float32 [4096, 16], P('blk'), may hold values from 1.7578125e-13 to 7.080078e-13
Outputs:
- norm_before: float32 [], replicated
- resid_norm: float32 [], replicated
- hidden_out: float32 [1024, 2048], P('blk', 'feat')
- hidden_moment_out: float32 [1024, 2048], P('blk', 'feat')
- hidden_second_out: float32 [1024, 2048], P('blk', 'feat')
- hidden_copy: bfloat16 [1024, 2048], P('blk', 'feat')
- alpha_out: float32 [4096, 16], P('blk')
- alpha_moment_out: float32 [4096, 16], P('blk')
- alpha_second_out: float32 [4096, 16], P('blk')
- alpha_copy: bfloat16 [4096, 16], P('blk')
All inputs are finite; a program needn't handle non-finite values.
Results may differ from a plain program's by a relative error of at most 0.0034.
Values may be sent and summed in bfloat16 or wider, within the bound.
No kernel may reach another device: no remote copies, remote signals or barrier semaphores. Data moves between devices by JAX's collectives and lax.ppermute only.
A program may use at most 192 MiB of HBM per device.

v0:
```python
import jax
import jax.numpy as jnp
from jax import lax
from jax.sharding import PartitionSpec as P

F = 2048
S = 16
ADAM_STEP = 10
PRECISE = lax.Precision.HIGHEST
NOISE = 0.01
CLIP_AT = 0.01
BETA_ONE = 0.9
BETA_TWO = 0.999
ADAM_EPS = 1e-08
DECAY = 0.01


def adamw_update(weight, moment, second, gradient, step_rate):
    moment = BETA_ONE * moment + (1.0 - BETA_ONE) * gradient
    second = BETA_TWO * second + (1.0 - BETA_TWO) * gradient * gradient
    moment_hat = moment / (1.0 - BETA_ONE**ADAM_STEP)
    second_hat = second / (1.0 - BETA_TWO**ADAM_STEP)
    weight = weight - step_rate * (moment_hat / (jnp.sqrt(second_hat) + ADAM_EPS) + DECAY * weight)
    return (weight, moment, second)


def kernel_step(features, pieces):
    kernel = jnp.einsum("tf,pf->tp", features, pieces[0], preferred_element_type=jnp.float32)
    fitted = jnp.dot(kernel, pieces[1].astype(jnp.float32), precision=PRECISE)
    summed = jnp.einsum("pf,ps->fs", pieces[0], pieces[1], preferred_element_type=jnp.float32)
    return (fitted, summed)


def on_device(
    inputs,
    col_mask,
    row_mask,
    width_class,
    frequencies,
    phases,
    targets,
    prior_draws,
    hidden_weight,
    hidden_moment,
    hidden_second,
    alpha_weight,
    alpha_moment,
    alpha_second,
):
    classes = col_mask.shape[0]
    feat_scale = (2.0 / F) ** 0.5
    onehot = (width_class[:, None] == jnp.arange(classes, dtype=jnp.int32)[None, :]).astype(
        jnp.float32
    )
    keep_cols = jnp.dot(onehot, col_mask.astype(jnp.float32))
    masked = inputs * keep_cols.astype(jnp.bfloat16)
    keep_rows = row_mask.astype(jnp.float32)
    true_count = jnp.maximum(lax.psum(jnp.sum(keep_rows), "blk"), 1.0)
    columns = masked
    first_pre = jnp.dot(
        columns,
        lax.all_gather(hidden_weight.astype(jnp.bfloat16), "blk", axis=0, tiled=True),
        preferred_element_type=jnp.float32,
    )
    tanh_full = jnp.tanh(first_pre)
    hidden = tanh_full.astype(jnp.bfloat16)
    pre = jnp.dot(
        lax.all_gather(hidden, "feat", axis=1, tiled=True),
        frequencies,
        preferred_element_type=jnp.float32,
    )
    phase_arg = pre + phases[None, :]
    features = (feat_scale * jnp.cos(phase_arg)).astype(jnp.bfloat16)
    alpha_low = alpha_weight.astype(jnp.bfloat16)

    def fold_step(pieces):
        return kernel_step(features, pieces)

    fitted_part, moments = fold_step(
        (
            lax.all_gather(features, "blk", axis=0, tiled=True),
            lax.all_gather(alpha_low, "blk", axis=0, tiled=True),
        )
    )
    fitted = lax.psum(fitted_part, "feat") + NOISE * alpha_weight
    residual = fitted - targets[:, None] - prior_draws
    resid_grad = (2.0 * keep_rows[:, None] * residual / (true_count * S)).astype(jnp.bfloat16)
    pulled_part, back_moments = fold_step(
        (
            lax.all_gather(features, "blk", axis=0, tiled=True),
            lax.all_gather(resid_grad, "blk", axis=0, tiled=True),
        )
    )
    alpha_grad = lax.psum(pulled_part, "feat") + NOISE * resid_grad.astype(jnp.float32)
    feature_grad = jnp.dot(resid_grad.astype(jnp.float32), moments.T, precision=PRECISE)
    feature_grad = feature_grad + jnp.dot(
        alpha_low.astype(jnp.float32), back_moments.T, precision=PRECISE
    )
    pre_grad = (-feat_scale * jnp.sin(phase_arg) * feature_grad).astype(jnp.bfloat16)
    hidden_terms = jnp.einsum(
        "tf,hf->th", pre_grad, frequencies, preferred_element_type=jnp.float32
    )
    hidden_grad = lax.psum_scatter(hidden_terms, "feat", scatter_dimension=1, tiled=True)
    first_grad = ((1.0 - tanh_full * tanh_full) * hidden_grad).astype(jnp.bfloat16)
    columns = masked
    weight_grad = lax.psum_scatter(
        jnp.einsum("td,th->dh", columns, first_grad, preferred_element_type=jnp.float32),
        "blk",
        scatter_dimension=0,
        tiled=True,
    )
    first_feat = (lax.axis_index("feat") == 0).astype(jnp.float32)
    grad_part = jnp.sum(weight_grad * weight_grad) + first_feat * jnp.sum(alpha_grad * alpha_grad)
    resid_part = first_feat * jnp.sum(keep_rows[:, None] * residual * residual)
    grad_total, resid_total = lax.psum((grad_part, resid_part), ("blk", "feat"))
    norm_before = jnp.sqrt(grad_total)
    resid_norm = jnp.sqrt(resid_total)
    clip = jnp.minimum(1.0, CLIP_AT / (norm_before + 1e-06))
    hidden_out, moment_out, second_out = adamw_update(
        hidden_weight, hidden_moment, hidden_second, weight_grad * clip, 0.02
    )
    alpha_out, alpha_moment_out, alpha_second_out = adamw_update(
        alpha_weight, alpha_moment, alpha_second, alpha_grad * clip, 0.05
    )
    return (
        norm_before,
        resid_norm,
        hidden_out,
        moment_out,
        second_out,
        hidden_out.astype(jnp.bfloat16),
        alpha_out,
        alpha_moment_out,
        alpha_second_out,
        alpha_out.astype(jnp.bfloat16),
    )


def solution(mesh):
    in_specs = (
        P("blk", None),
        P(),
        P("blk"),
        P("blk"),
        P(None, "feat"),
        P("feat"),
        P("blk"),
        P("blk", None),
        P("blk", "feat"),
        P("blk", "feat"),
        P("blk", "feat"),
        P("blk", None),
        P("blk", None),
        P("blk", None),
    )
    out_specs = (
        P(),
        P(),
        P("blk", "feat"),
        P("blk", "feat"),
        P("blk", "feat"),
        P("blk", "feat"),
        P("blk", None),
        P("blk", None),
        P("blk", None),
        P("blk", None),
    )
    return jax.shard_map(
        on_device, mesh=mesh, in_specs=in_specs, out_specs=out_specs, check_vma=False
    )
```

profile of v0, /device:TPU:0, one launch (start us, length us, event | category | flops | bytes accessed | tf_op | source)
XLA Modules:
  0.0 378.5 jit_solution(18336091625798306020)
XLA Ops:
  7.2 0.0 copy-start.11
  7.2 0.0 all-gather.4.cloned.1.call-start
  7.2 1.6 convert_element_type.47
  8.9 0.0 all-gather.4.cloned.1.call-update
  8.9 0.0 all-gather.6.cloned.1.call-start
  8.9 1.4 fusion.3
  10.3 44.6 %all-gather.4.cloned.1.call-done = bf16[1024,1024]{1,0:T(8,128)(2,1)} async-done(((bf16[64,1024]{1,0:T(8,128)(2,1)}), bf16[1024,1024]{1,0:T(8,128)(2,1)}) %all-gather.4.cloned.1.call-update) | async-done | bytes 2097168 | tf_op jit(solution)/shard_map/all_gather | solution.py:62
  54.9 3.1 fusion.16
  58.1 0.0 all-gather.6.cloned.1.call-update
  58.1 0.0 copy-start.8
  58.1 0.0 copy-start.4
  58.1 0.0 all-gather.8.cloned.1.call-start
  58.2 20.1 %all-gather.6.cloned.1.call-done = bf16[256,2048]{1,0:T(8,128)(2,1)} async-done(((bf16[256,1024]{1,0:T(8,128)(2,1)}), bf16[256,2048]{1,0:T(8,128)(2,1)}) %all-gather.6.cloned.1.call-update) | async-done | bytes 1048592 | tf_op jit(solution)/shard_map/all_gather | solution.py:68
  78.3 0.0 copy-done.11
  78.3 7.3 %multiply_convert_fusion.1 = (bf16[256,1024]{1,0:T(8,128)(2,1)}, f32[256,1024]{1,0:T(8,128)S(1)}) fusion(f32[1024]{0:T(1024)S(1)} %copy-done.11, bf16[256,2048]{1,0:T(8,128)(2,1)} %all-gather.6.cloned.1.call-done, bf16[2048,1024]{1,0:T(8,128)(2,1)} %param.18), kind=kOutput, calls=%fused_computation.9 | convolution fusion | flops 1074528256 | bytes 6819840 | tf_op jit(solution)/shard_map/dot_general | solution.py:67
  85.6 0.0 all-gather.8.cloned.1.call-update
  85.6 0.0 reduce-scatter.3.cloned.1.call-start
  85.6 0.0 copy-done.8
  85.6 0.6 broadcast_multiply_fusion
  86.2 34.6 %psum.36 = f32[]{:T(128)} all-reduce(f32[]{:T(128)} %get-tuple-element.23), channel_id=1, replica_groups=mesh['blk'=16,'feat'=2] {'blk'}, use_global_device_ids=true, to_apply=%region_2.0 | all-reduce | flops 1 | bytes 8 | tf_op jit(solution)/shard_map/psum | solution.py:58
  120.8 0.0 copy-done.4
  121.5 18.8 %all_gather.19 = bf16[4096,16]{0,1:T(8,128)(2,1)S(1)} all-gather(bf16[256,16]{0,1:T(8,128)(2,1)S(1)} %convert_element_type.51), channel_id=1, replica_groups=mesh['blk'=16,'feat'=2] {'blk'}, dimensions={0}, use_global_device_ids=true | all-gather | bytes 139264 | tf_op jit(solution)/shard_map/all_gather | solution.py:82
  140.2 20.7 %all-gather.8.cloned.1.call-done = bf16[4096,1024]{1,0:T(8,128)(2,1)} async-done(((bf16[256,1024]{1,0:T(8,128)(2,1)}), bf16[4096,1024]{1,0:T(8,128)(2,1)}) %all-gather.8.cloned.1.call-update) | async-done | bytes 8388624 | tf_op jit(solution)/shard_map/all_gather | solution.py:81
  160.9 5.9 %fusion.17 = f32[256,4096]{1,0:T(8,128)S(1)} fusion(bf16[256,1024]{1,0:T(8,128)(2,1)} %get-tuple-element.26, bf16[4096,1024]{1,0:T(8,128)(2,1)} %all-gather.8.cloned.1.call-done), kind=kOutput, calls=%fused_computation.36 | convolution fusion | flops 2147483648 | bytes 13107200 | tf_op jit(solution)/shard_map/tf,pf->tp/dot_general | solution.py:28
  166.9 0.0 copy-start
  166.9 1.9 copy-done
  168.8 0.0 copy-start.7
  168.8 0.0 copy-start.9
  168.8 2.0 fusion.18
  170.8 8.3 %psum.35 = f32[256,16]{0,1:T(8,128)S(1)} all-reduce(f32[256,16]{0,1:T(8,128)S(1)} %fusion.18), channel_id=1, replica_groups=mesh['blk'=16,'feat'=2] {'feat'}, use_global_device_ids=true, to_apply=%region_0.0 | all-reduce | flops 4096 | bytes 32768 | tf_op jit(solution)/shard_map/psum | solution.py:85
  179.2 0.0 copy-done.7
  179.2 0.0 copy-done.9
  179.2 0.6 fusion.8
  179.8 19.3 %all_gather.20 = bf16[4096,16]{0,1:T(8,128)(2,1)S(1)} all-gather(bf16[256,16]{0,1:T(8,128)(2,1)S(1)} %divide_convert_fusion), channel_id=1, replica_groups=mesh['blk'=16,'feat'=2] {'blk'}, dimensions={0}, use_global_device_ids=true | all-gather | bytes 139264 | tf_op jit(solution)/shard_map/all_gather | solution.py:91
  199.1 5.8 %fusion.19 = f32[1024,16]{1,0:T(8,128)S(1)} fusion(bf16[4096,1024]{1,0:T(8,128)(2,1)} %all-gather.8.cloned.1.call-done, bf16[4096,16]{0,1:T(8,128)(2,1)S(1)} %all_gather.19), kind=kOutput, calls=%fused_computation.38 | convolution fusion | flops 134217728 | bytes 8585216 | tf_op jit(solution)/shard_map/pf,ps->fs/dot_general | solution.py:30
  204.8 0.6 fusion.20
  205.5 0.0 copy-start.10
  205.5 5.9 %fusion.21 = f32[1024,16]{1,0:T(8,128)S(1)} fusion(bf16[4096,1024]{1,0:T(8,128)(2,1)} %all-gather.8.cloned.1.call-done, bf16[4096,16]{0,1:T(8,128)(2,1)S(1)} %all_gather.20), kind=kOutput, calls=%fused_computation.40 | convolution fusion | flops 134217728 | bytes 8585216 | tf_op jit(solution)/shard_map/pf,ps->fs/dot_general | solution.py:30
  211.4 4.3 %fusion.2 = bf16[256,1024]{1,0:T(8,128)(2,1)S(1)} fusion(f32[256,1024]{1,0:T(8,128)S(1)} %fusion.20, f32[1024,16]{1,0:T(8,128)S(1)} %fusion.21, bf16[256,16]{0,1:T(8,128)(2,1)S(1)} %convert_element_type.51, f32[256,1024]{1,0:T(8,128)S(1)} %get-tuple-element.27), kind=kOutput, calls=%fused_computation.5 | convolution fusion | flops 51380224 | bytes 2695168 | tf_op jit(solution)/shard_map/dot_general | solution.py:96
  215.7 0.0 copy-done.10
  215.7 2.6 fusion.22
  218.3 0.0 reduce-scatter.3.cloned.1.call-update
  218.3 0.0 reduce-scatter.5.cloned.1.call-start
  218.4 28.4 %reduce-scatter.3.cloned.1.call-done = f32[256,1024]{1,0:T(8,128)} async-done(((f32[256,2048]{1,0:T(8,128)}), f32[256,1024]{1,0:T(8,128)}) %reduce-scatter.3.cloned.1.call-update) | async-done | bytes 1048592 | tf_op jit(solution)/shard_map/reduce_scatter | solution.py:103
  246.8 3.9 %fusion.4 = f32[1024,1024]{1,0:T(8,128)} fusion(bf16[256,1024]{1,0:T(8,128)(2,1)S(1)} %fusion.3, f32[256,1024]{1,0:T(8,128)} %reduce-scatter.3.cloned.1.call-done, f32[256,1024]{1,0:T(8,128)S(1)} %get-tuple-element.25), kind=kOutput, calls=%fused_computation.10 | convolution fusion | flops 537919488 | bytes 6815744 | tf_op jit(solution)/shard_map/td,th->dh/dot_general | solution.py:107
  250.8 0.0 copy-start.5
  250.8 0.0 copy-start.6
  250.8 0.0 copy-start.1
  250.8 0.0 copy-start.2
  250.8 0.0 copy-start.3
  250.8 0.0 reduce-scatter.5.cloned.1.call-update
  251.5 4.2 %fusion.23 = f32[256,16]{0,1:T(8,128)S(1)} fusion(f32[256,4096]{1,0:T(8,128)} %copy-done, bf16[4096,16]{0,1:T(8,128)(2,1)S(1)} %all_gather.20), kind=kOutput, calls=%fused_computation.42 | convolution fusion | flops 201326592 | bytes 4341760 | tf_op jit(solution)/shard_map/dot_general | solution.py:29
  255.7 7.0 %psum.37 = f32[256,16]{0,1:T(8,128)S(1)} all-reduce(f32[256,16]{0,1:T(8,128)S(1)} %fusion.23), channel_id=1, replica_groups=mesh['blk'=16,'feat'=2] {'feat'}, use_global_device_ids=true, to_apply=%region_6.0 | all-reduce | flops 4096 | bytes 32768 | tf_op jit(solution)/shard_map/psum | solution.py:94
  262.7 0.6 multiply_reduce_fusion.1
  264.0 59.8 %reduce-scatter.5.cloned.1.call-done = f32[64,1024]{1,0:T(8,128)} async-done(((f32[1024,1024]{1,0:T(8,128)}), f32[64,1024]{1,0:T(8,128)}) %reduce-scatter.5.cloned.1.call-update) | async-done | bytes 262160 | tf_op jit(solution)/shard_map/reduce_scatter | solution.py:106
  323.7 1.6 multiply_reduce_fusion
  326.0 39.6 %all-reduce = (f32[]{:T(128)}, f32[]{:T(128)}) all-reduce(f32[]{:T(128)S(6)} %add.72, f32[]{:T(128)S(6)} %mul.177), channel_id=1, replica_groups=mesh['blk'=16,'feat'=2] {'blk','feat'}, use_global_device_ids=true, to_apply=%region_8.0 | all-reduce | flops 2 | bytes 16 | tf_op jit(solution)/shard_map/psum | solution.py:115
  367.0 0.0 copy-done.5
  367.0 0.0 copy-done.6
  367.0 0.6 fusion.12
  367.7 0.0 copy-done.1
  367.7 0.0 copy-done.2
  367.7 0.0 copy-done.3
  367.7 2.0 fusion.14
  (3 shorter events, 0.0 us)
Async XLA Ops:
  7.2 71.1 %copy-start.11 = (f32[1024]{0:T(1024)S(1)}, f32[1024]{0:T(1024)}, u32[]{:S(2)}) copy-start(f32[1024]{0:T(1024)} %param.19) | copy-start | bytes 12292
  7.2 47.8 %all-gather.4.cloned.1.call-start = ((), (), s32[]{:S(2)}) async-start(), calls=%async_computation.2 | async-start | bytes 2228224 | tf_op jit(solution)/shard_map/all_gather | solution.py:62
  8.9 69.4 %all-gather.6.cloned.1.call-start = ((), (), s32[]{:S(2)}) async-start(), calls=%async_computation.3 | async-start | bytes 1572864 | tf_op jit(solution)/shard_map/all_gather | solution.py:68
  58.1 27.5 %copy-start.8 = (s32[256]{0:T(256)S(1)}, s32[256]{0:T(256)}, u32[]{:S(2)}) copy-start(s32[256]{0:T(256)} %param.16) | copy-start | bytes 3076
  58.1 62.7 %copy-start.4 = (f32[256,16]{0,1:T(8,128)S(1)}, f32[256,16]{0,1:T(8,128)}, u32[]{:S(2)}) copy-start(f32[256,16]{0,1:T(8,128)} %param.25) | copy-start | bytes 49156
  58.1 102.8 %all-gather.8.cloned.1.call-start = ((), (), s32[]{:S(2)}) async-start(), calls=%async_computation.4 | async-start | bytes 8912896 | tf_op jit(solution)/shard_map/all_gather | solution.py:81
  85.6 161.2 %reduce-scatter.3.cloned.1.call-start = ((), (), s32[]{:S(2)}) async-start(), calls=%async_computation.5 | async-start | bytes 3145728 | tf_op jit(solution)/shard_map/reduce_scatter | solution.py:103
  166.9 1.9 copy-start
  168.8 10.3 %copy-start.7 = (f32[256,16]{0,1:T(8,128)S(1)}, f32[256,16]{0,1:T(8,128)}, u32[]{:S(2)}) copy-start(f32[256,16]{0,1:T(8,128)} %param.21) | copy-start | bytes 49156
  168.8 10.3 %copy-start.9 = (f32[256]{0:T(256)S(1)}, f32[256]{0:T(256)}, u32[]{:S(2)}) copy-start(f32[256]{0:T(256)} %param.20) | copy-start | bytes 3076
  205.5 10.2 %copy-start.10 = (bf16[2048,1024]{1,0:T(8,128)(2,1)S(1)}, bf16[2048,1024]{1,0:T(8,128)(2,1)}, u32[]{:S(2)}) copy-start(bf16[2048,1024]{1,0:T(8,128)(2,1)} %param.18) | copy-start | bytes 12582916
  218.3 105.4 %reduce-scatter.5.cloned.1.call-start = ((), (), s32[]{:S(2)}) async-start(), calls=%async_computation.6 | async-start | bytes 4456448 | tf_op jit(solution)/shard_map/reduce_scatter | solution.py:106
  250.8 116.3 %copy-start.5 = (f32[256,16]{0,1:T(8,128)S(1)}, f32[256,16]{0,1:T(8,128)}, u32[]{:S(2)}) copy-start(f32[256,16]{0,1:T(8,128)} %param.26) | copy-start | bytes 49156
  250.8 116.3 %copy-start.6 = (f32[256,16]{0,1:T(8,128)S(1)}, f32[256,16]{0,1:T(8,128)}, u32[]{:S(2)}) copy-start(f32[256,16]{0,1:T(8,128)} %param.27) | copy-start | bytes 49156
  250.8 116.9 %copy-start.1 = (f32[64,1024]{1,0:T(8,128)S(1)}, f32[64,1024]{1,0:T(8,128)}, u32[]{:S(2)}) copy-start(f32[64,1024]{1,0:T(8,128)} %param.22) | copy-start | bytes 786436
  250.8 116.9 %copy-start.2 = (f32[64,1024]{1,0:T(8,128)S(1)}, f32[64,1024]{1,0:T(8,128)}, u32[]{:S(2)}) copy-start(f32[64,1024]{1,0:T(8,128)} %param.23) | copy-start | bytes 786436
  250.8 116.9 %copy-start.3 = (f32[64,1024]{1,0:T(8,128)S(1)}, f32[64,1024]{1,0:T(8,128)}, u32[]{:S(2)}) copy-start(f32[64,1024]{1,0:T(8,128)} %param.24) | copy-start | bytes 786436
Sparse Core Ops, SparseCore 0:
  10.7 44.1 all-gather.3
  58.2 19.9 all-gather.5
  85.7 75.1 all-gather.7
  218.4 28.3 reduce-scatter.2
  250.9 72.7 reduce-scatter.4
where the time goes:
time: 379 us; the launch traced here: 378 us
  waiting for transfers between devices  174 us (46%)
  blocking collectives  128 us (34%)
  matrix products  47.1 us (12%)
  between operations  20.3 us (5%)
  other arithmetic  7.74 us (2%)
    reduce_scatter x1, waiting for transfers between devices, on_device(): lax.psum_scatter(jnp.einsum('td,th->dh', columns, first_grad, preferred_e...  59.8 us
    all_gather x1, waiting for transfers between devices, on_device(): lax.all_gather(hidden_weight.astype(jnp.bfloat16), 'blk', axis=0, tiled=T...  44.6 us
    psum x1, blocking collectives, on_device(): grad_total, resid_total = lax.psum((grad_part, resid_part), ('blk', 'feat'))  39.6 us
    psum x1, blocking collectives, on_device(): true_count = jnp.maximum(lax.psum(jnp.sum(keep_rows), 'blk'), 1.0)  34.6 us
    reduce_scatter x1, waiting for transfers between devices, on_device(): lax.psum_scatter(hidden_terms, 'feat', scatter_dimension=1, tiled=True)  28.4 us
    all_gather x1, waiting for transfers between devices, on_device(): lax.all_gather(features, 'blk', axis=0, tiled=True)  20.7 us
    all_gather x1, waiting for transfers between devices, on_device(): lax.all_gather(hidden, 'feat', axis=1, tiled=True)  20.1 us
    all_gather x1, blocking collectives, on_device(): lax.all_gather(resid_grad, 'blk', axis=0, tiled=True)  19.3 us
  transfers between devices with their start and end apart: 5, of which 5 were waited for; matrix products, arithmetic and copies ran while one was open for 2% of the time, Pallas kernels for 0%

commit v1 on v0

--- a/solution.py
+++ b/solution.py
@@ -82,7 +82,7 @@
             lax.all_gather(alpha_low, "blk", axis=0, tiled=True),
         )
     )
-    fitted = lax.psum(fitted_part, "feat") + NOISE * alpha_weight
+    fitted = jnp.sum(lax.all_gather(fitted_part, "feat"), axis=0) + NOISE * alpha_weight
     residual = fitted - targets[:, None] - prior_draws
     resid_grad = (2.0 * keep_rows[:, None] * residual / (true_count * S)).astype(jnp.bfloat16)
     pulled_part, back_moments = fold_step(

time: 379 us -> 376 us (level)
  blocking collectives: 128 us -> 124 us
    psum x1 -> x0, blocking collectives: 8.33 us -> none  [on_device(): fitted = lax.psum(fitted_part, 'feat') + NOISE * alpha_weight]
    all_gather x0 -> x1, blocking collectives: none -> 4.42 us  [on_device(): lax.all_gather(fitted_part, 'feat')]
where the time goes in v1:
time: 376 us
  waiting for transfers between devices  174 us (46%)
  blocking collectives  124 us (33%)
  matrix products  47.1 us (13%)
  between operations  20.3 us (5%)
  other arithmetic  7.78 us (2%)
    reduce_scatter x1, waiting for transfers between devices, on_device(): lax.psum_scatter(jnp.einsum('td,th->dh', columns, first_grad, preferred_e...  59.8 us
    all_gather x1, waiting for transfers between devices, on_device(): lax.all_gather(hidden_weight.astype(jnp.bfloat16), 'blk', axis=0, tiled=T...  44.6 us
    psum x1, blocking collectives, on_device(): grad_total, resid_total = lax.psum((grad_part, resid_part), ('blk', 'feat'))  39.5 us
    psum x1, blocking collectives, on_device(): true_count = jnp.maximum(lax.psum(jnp.sum(keep_rows), 'blk'), 1.0)  34.6 us
    reduce_scatter x1, waiting for transfers between devices, on_device(): lax.psum_scatter(hidden_terms, 'feat', scatter_dimension=1, tiled=True)  29.1 us
    all_gather x1, waiting for transfers between devices, on_device(): lax.all_gather(features, 'blk', axis=0, tiled=True)  20.7 us
    all_gather x1, waiting for transfers between devices, on_device(): lax.all_gather(hidden, 'feat', axis=1, tiled=True)  20.1 us
    all_gather x1, blocking collectives, on_device(): lax.all_gather(resid_grad, 'blk', axis=0, tiled=True)  19.6 us
  transfers between devices with their start and end apart: 5, of which 5 were waited for; matrix products, arithmetic and copies ran while one was open for 2% of the time, Pallas kernels for 0%

profile of v1, /device:TPU:0, one launch (start us, length us, event | category | flops | bytes accessed | tf_op | source)
XLA Modules:
  0.0 375.7 jit_solution(3853858654798396619)
XLA Ops:
  7.2 0.0 copy-start.11
  7.2 0.0 all-gather.5.cloned.1.call-start
  7.2 1.6 convert_element_type.47
  8.9 0.0 all-gather.5.cloned.1.call-update
  8.9 0.0 all-gather.7.cloned.1.call-start
  8.9 1.4 fusion.3
  10.3 44.6 %all-gather.5.cloned.1.call-done = bf16[1024,1024]{1,0:T(8,128)(2,1)} async-done(((bf16[64,1024]{1,0:T(8,128)(2,1)}), bf16[1024,1024]{1,0:T(8,128)(2,1)}) %all-gather.5.cloned.1.call-update) | async-done | bytes 2097168 | tf_op jit(solution)/shard_map/all_gather | solution.py:62
  54.9 3.1 fusion.16
  58.1 0.0 all-gather.7.cloned.1.call-update
  58.1 0.0 copy-start.8
  58.1 0.0 copy-start.4
  58.1 0.0 all-gather.9.cloned.1.call-start
  58.2 20.1 %all-gather.7.cloned.1.call-done = bf16[256,2048]{1,0:T(8,128)(2,1)} async-done(((bf16[256,1024]{1,0:T(8,128)(2,1)}), bf16[256,2048]{1,0:T(8,128)(2,1)}) %all-gather.7.cloned.1.call-update) | async-done | bytes 1048592 | tf_op jit(solution)/shard_map/all_gather | solution.py:68
  78.3 0.0 copy-done.11
  78.3 7.3 %multiply_convert_fusion.1 = (bf16[256,1024]{1,0:T(8,128)(2,1)}, f32[256,1024]{1,0:T(8,128)S(1)}) fusion(f32[1024]{0:T(1024)S(1)} %copy-done.11, bf16[256,2048]{1,0:T(8,128)(2,1)} %all-gather.7.cloned.1.call-done, bf16[2048,1024]{1,0:T(8,128)(2,1)} %param.18), kind=kOutput, calls=%fused_computation.9 | convolution fusion | flops 1074528256 | bytes 6819840 | tf_op jit(solution)/shard_map/dot_general | solution.py:67
  85.6 0.0 all-gather.9.cloned.1.call-update
  85.6 0.0 reduce-scatter.3.cloned.1.call-start
  85.6 0.0 copy-done.8
  85.6 0.6 broadcast_multiply_fusion
  86.2 34.6 %psum.28 = f32[]{:T(128)} all-reduce(f32[]{:T(128)} %get-tuple-element.23), channel_id=1, replica_groups=mesh['blk'=16,'feat'=2] {'blk'}, use_global_device_ids=true, to_apply=%region_2.0 | all-reduce | flops 1 | bytes 8 | tf_op jit(solution)/shard_map/psum | solution.py:58
  120.8 0.0 copy-done.4
  121.5 18.8 %all_gather.25 = bf16[4096,16]{0,1:T(8,128)(2,1)S(1)} all-gather(bf16[256,16]{0,1:T(8,128)(2,1)S(1)} %convert_element_type.51), channel_id=1, replica_groups=mesh['blk'=16,'feat'=2] {'blk'}, dimensions={0}, use_global_device_ids=true | all-gather | bytes 139264 | tf_op jit(solution)/shard_map/all_gather | solution.py:82
  140.2 20.7 %all-gather.9.cloned.1.call-done = bf16[4096,1024]{1,0:T(8,128)(2,1)} async-done(((bf16[256,1024]{1,0:T(8,128)(2,1)}), bf16[4096,1024]{1,0:T(8,128)(2,1)}) %all-gather.9.cloned.1.call-update) | async-done | bytes 8388624 | tf_op jit(solution)/shard_map/all_gather | solution.py:81
  160.9 5.9 %fusion.17 = f32[256,4096]{1,0:T(8,128)S(1)} fusion(bf16[256,1024]{1,0:T(8,128)(2,1)} %get-tuple-element.26, bf16[4096,1024]{1,0:T(8,128)(2,1)} %all-gather.9.cloned.1.call-done), kind=kOutput, calls=%fused_computation.36 | convolution fusion | flops 2147483648 | bytes 13107200 | tf_op jit(solution)/shard_map/tf,pf->tp/dot_general | solution.py:28
  166.9 0.0 copy-start
  166.9 1.9 copy-done
  168.8 0.0 copy-start.7
  168.8 0.0 copy-start.9
  168.8 2.0 fusion.18
  170.8 4.4 %all-gather = f32[512,16]{0,1:T(8,128)S(1)} all-gather(f32[256,16]{0,1:T(8,128)S(1)} %fusion.18), channel_id=2, replica_groups=mesh['blk'=16,'feat'=2] {'feat'}, dimensions={0}, use_global_device_ids=true | all-gather | bytes 49152 | tf_op jit(solution)/shard_map/all_gather | solution.py:85
  175.3 0.0 copy-done.7
  175.3 0.0 copy-done.9
  175.3 0.6 fusion.8
  176.0 19.6 %all_gather.28 = bf16[4096,16]{0,1:T(8,128)(2,1)S(1)} all-gather(bf16[256,16]{0,1:T(8,128)(2,1)S(1)} %divide_convert_fusion), channel_id=1, replica_groups=mesh['blk'=16,'feat'=2] {'blk'}, dimensions={0}, use_global_device_ids=true | all-gather | bytes 139264 | tf_op jit(solution)/shard_map/all_gather | solution.py:91
  195.6 5.8 %fusion.19 = f32[1024,16]{1,0:T(8,128)S(1)} fusion(bf16[4096,1024]{1,0:T(8,128)(2,1)} %all-gather.9.cloned.1.call-done, bf16[4096,16]{0,1:T(8,128)(2,1)S(1)} %all_gather.25), kind=kOutput, calls=%fused_computation.38 | convolution fusion | flops 134217728 | bytes 8585216 | tf_op jit(solution)/shard_map/pf,ps->fs/dot_general | solution.py:30
  201.3 0.6 fusion.20
  201.9 0.0 copy-start.10
  202.0 5.9 %fusion.21 = f32[1024,16]{1,0:T(8,128)S(1)} fusion(bf16[4096,1024]{1,0:T(8,128)(2,1)} %all-gather.9.cloned.1.call-done, bf16[4096,16]{0,1:T(8,128)(2,1)S(1)} %all_gather.28), kind=kOutput, calls=%fused_computation.40 | convolution fusion | flops 134217728 | bytes 8585216 | tf_op jit(solution)/shard_map/pf,ps->fs/dot_general | solution.py:30
  207.9 4.3 %fusion.2 = bf16[256,1024]{1,0:T(8,128)(2,1)S(1)} fusion(f32[256,1024]{1,0:T(8,128)S(1)} %fusion.20, f32[1024,16]{1,0:T(8,128)S(1)} %fusion.21, bf16[256,16]{0,1:T(8,128)(2,1)S(1)} %convert_element_type.51, f32[256,1024]{1,0:T(8,128)S(1)} %get-tuple-element.27), kind=kOutput, calls=%fused_computation.5 | convolution fusion | flops 51380224 | bytes 2695168 | tf_op jit(solution)/shard_map/dot_general | solution.py:96
  212.1 0.0 copy-done.10
  212.2 2.6 fusion.22
  214.8 0.0 reduce-scatter.3.cloned.1.call-update
  214.8 0.0 reduce-scatter.5.cloned.1.call-start
  214.9 29.1 %reduce-scatter.3.cloned.1.call-done = f32[256,1024]{1,0:T(8,128)} async-done(((f32[256,2048]{1,0:T(8,128)}), f32[256,1024]{1,0:T(8,128)}) %reduce-scatter.3.cloned.1.call-update) | async-done | bytes 1048592 | tf_op jit(solution)/shard_map/reduce_scatter | solution.py:103
  244.0 3.9 %fusion.4 = f32[1024,1024]{1,0:T(8,128)} fusion(bf16[256,1024]{1,0:T(8,128)(2,1)S(1)} %fusion.3, f32[256,1024]{1,0:T(8,128)} %reduce-scatter.3.cloned.1.call-done, f32[256,1024]{1,0:T(8,128)S(1)} %get-tuple-element.25), kind=kOutput, calls=%fused_computation.10 | convolution fusion | flops 537919488 | bytes 6815744 | tf_op jit(solution)/shard_map/td,th->dh/dot_general | solution.py:107
  247.9 0.0 copy-start.5
  247.9 0.0 copy-start.6
  247.9 0.0 copy-start.1
  247.9 0.0 copy-start.2
  247.9 0.0 copy-start.3
  247.9 0.0 reduce-scatter.5.cloned.1.call-update
  248.7 4.2 %fusion.23 = f32[256,16]{0,1:T(8,128)S(1)} fusion(f32[256,4096]{1,0:T(8,128)} %copy-done, bf16[4096,16]{0,1:T(8,128)(2,1)S(1)} %all_gather.28), kind=kOutput, calls=%fused_computation.42 | convolution fusion | flops 201326592 | bytes 4341760 | tf_op jit(solution)/shard_map/dot_general | solution.py:29
  252.9 7.0 %psum.29 = f32[256,16]{0,1:T(8,128)S(1)} all-reduce(f32[256,16]{0,1:T(8,128)S(1)} %fusion.23), channel_id=1, replica_groups=mesh['blk'=16,'feat'=2] {'feat'}, use_global_device_ids=true, to_apply=%region_6.0 | all-reduce | flops 4096 | bytes 32768 | tf_op jit(solution)/shard_map/psum | solution.py:94
  259.9 0.6 multiply_reduce_fusion.1
  261.1 59.8 %reduce-scatter.5.cloned.1.call-done = f32[64,1024]{1,0:T(8,128)} async-done(((f32[1024,1024]{1,0:T(8,128)}), f32[64,1024]{1,0:T(8,128)}) %reduce-scatter.5.cloned.1.call-update) | async-done | bytes 262160 | tf_op jit(solution)/shard_map/reduce_scatter | solution.py:106
  321.0 1.6 multiply_reduce_fusion
  323.3 39.5 %all-reduce = (f32[]{:T(128)}, f32[]{:T(128)}) all-reduce(f32[]{:T(128)S(6)} %add.70, f32[]{:T(128)S(6)} %mul.177), channel_id=1, replica_groups=mesh['blk'=16,'feat'=2] {'blk','feat'}, use_global_device_ids=true, to_apply=%region_8.0 | all-reduce | flops 2 | bytes 16 | tf_op jit(solution)/shard_map/psum | solution.py:115
  364.2 0.0 copy-done.5
  364.2 0.0 copy-done.6
  364.2 0.6 fusion.12
  364.9 0.0 copy-done.1
  364.9 0.0 copy-done.2
  364.9 0.0 copy-done.3
  364.9 2.0 fusion.14
  (5 shorter events, 0.1 us)
Async XLA Ops:
  7.2 71.1 %copy-start.11 = (f32[1024]{0:T(1024)S(1)}, f32[1024]{0:T(1024)}, u32[]{:S(2)}) copy-start(f32[1024]{0:T(1024)} %param.19) | copy-start | bytes 12292
  7.2 47.8 %all-gather.5.cloned.1.call-start = ((), (), s32[]{:S(2)}) async-start(), calls=%async_computation.2 | async-start | bytes 2228224 | tf_op jit(solution)/shard_map/all_gather | solution.py:62
  8.9 69.4 %all-gather.7.cloned.1.call-start = ((), (), s32[]{:S(2)}) async-start(), calls=%async_computation.3 | async-start | bytes 1572864 | tf_op jit(solution)/shard_map/all_gather | solution.py:68
  58.1 27.5 %copy-start.8 = (s32[256]{0:T(256)S(1)}, s32[256]{0:T(256)}, u32[]{:S(2)}) copy-start(s32[256]{0:T(256)} %param.16) | copy-start | bytes 3076
  58.1 62.7 %copy-start.4 = (f32[256,16]{0,1:T(8,128)S(1)}, f32[256,16]{0,1:T(8,128)}, u32[]{:S(2)}) copy-start(f32[256,16]{0,1:T(8,128)} %param.25) | copy-start | bytes 49156
  58.1 102.8 %all-gather.9.cloned.1.call-start = ((), (), s32[]{:S(2)}) async-start(), calls=%async_computation.4 | async-start | bytes 8912896 | tf_op jit(solution)/shard_map/all_gather | solution.py:81
  85.6 158.4 %reduce-scatter.3.cloned.1.call-start = ((), (), s32[]{:S(2)}) async-start(), calls=%async_computation.5 | async-start | bytes 3145728 | tf_op jit(solution)/shard_map/reduce_scatter | solution.py:103
  166.9 1.9 copy-start
  168.8 6.5 %copy-start.7 = (f32[256,16]{0,1:T(8,128)S(1)}, f32[256,16]{0,1:T(8,128)}, u32[]{:S(2)}) copy-start(f32[256,16]{0,1:T(8,128)} %param.21) | copy-start | bytes 49156
  168.8 6.5 %copy-start.9 = (f32[256]{0:T(256)S(1)}, f32[256]{0:T(256)}, u32[]{:S(2)}) copy-start(f32[256]{0:T(256)} %param.20) | copy-start | bytes 3076
  201.9 10.2 %copy-start.10 = (bf16[2048,1024]{1,0:T(8,128)(2,1)S(1)}, bf16[2048,1024]{1,0:T(8,128)(2,1)}, u32[]{:S(2)}) copy-start(bf16[2048,1024]{1,0:T(8,128)(2,1)} %param.18) | copy-start | bytes 12582916
  214.8 106.2 %reduce-scatter.5.cloned.1.call-start = ((), (), s32[]{:S(2)}) async-start(), calls=%async_computation.6 | async-start | bytes 4456448 | tf_op jit(solution)/shard_map/reduce_scatter | solution.py:106
  247.9 116.3 %copy-start.5 = (f32[256,16]{0,1:T(8,128)S(1)}, f32[256,16]{0,1:T(8,128)}, u32[]{:S(2)}) copy-start(f32[256,16]{0,1:T(8,128)} %param.26) | copy-start | bytes 49156
  247.9 116.3 %copy-start.6 = (f32[256,16]{0,1:T(8,128)S(1)}, f32[256,16]{0,1:T(8,128)}, u32[]{:S(2)}) copy-start(f32[256,16]{0,1:T(8,128)} %param.27) | copy-start | bytes 49156
  247.9 117.0 %copy-start.1 = (f32[64,1024]{1,0:T(8,128)S(1)}, f32[64,1024]{1,0:T(8,128)}, u32[]{:S(2)}) copy-start(f32[64,1024]{1,0:T(8,128)} %param.22) | copy-start | bytes 786436
  247.9 117.0 %copy-start.2 = (f32[64,1024]{1,0:T(8,128)S(1)}, f32[64,1024]{1,0:T(8,128)}, u32[]{:S(2)}) copy-start(f32[64,1024]{1,0:T(8,128)} %param.23) | copy-start | bytes 786436
  247.9 117.0 %copy-start.3 = (f32[64,1024]{1,0:T(8,128)S(1)}, f32[64,1024]{1,0:T(8,128)}, u32[]{:S(2)}) copy-start(f32[64,1024]{1,0:T(8,128)} %param.24) | copy-start | bytes 786436
Sparse Core Ops, SparseCore 0:
  10.7 44.1 all-gather.4
  58.2 19.9 all-gather.6
  85.7 75.1 all-gather.8
  214.9 29.0 reduce-scatter.2
  248.1 72.8 reduce-scatter.4
